TPU v7x, 256 devices: a whole 4x4x8 slice. The times are simulated.
256 devices in a mesh: dp: 8 (over x, core), tm: 32 (over z, y).
Axes of the slice: x: 4, y: 4, z: 8, core: 2. Of those that a mesh axis runs over, the one named last changes fastest.
Arguments:
- latents: bfloat16 [8, 17, 64, 64, 256], P('dp', None, 'tm'), may hold values from -6 to 6
- cotangent: bfloat16 [8, 17, 64, 64, 256], P('dp', None, 'tm'), may hold values from -6 to 6
- spatial_weight: bfloat16 [3, 3, 256, 256], replicated, may hold values from -0.125 to 0.125
- temporal_weight: bfloat16 [3, 256, 256], replicated, may hold values from -0.21875 to 0.21875
Outputs:
- block_out: bfloat16 [8, 17, 64, 64, 256], P('dp', None, 'tm')
- latents_grad: bfloat16 [8, 17, 64, 64, 256], P('dp', None, 'tm')
- spatial_grad: float32 [3, 3, 256, 256], replicated
- temporal_grad: float32 [3, 256, 256], replicated
All inputs are finite; a program needn't handle non-finite values.
Results may differ from a plain program's by a relative error of at most 0.0085.
Values may be sent and summed in bfloat16 or wider, within the bound.
A program may use at most 64 MiB of HBM per device.

v0:
```python
import jax
import jax.numpy as jnp
from jax import lax
from jax.sharding import PartitionSpec as P


def with_halo(cells, sides, width):
    for axis, dim in sides:
        count = lax.axis_size(axis)
        ends = count - 1
        head = lax.slice_in_dim(cells, 0, width, axis=dim)
        tail = lax.slice_in_dim(cells, cells.shape[dim] - width, cells.shape[dim], axis=dim)
        cells = jnp.concatenate(
            [
                lax.ppermute(tail, axis, [(i, (i + 1) % count) for i in range(ends)]),
                cells,
                lax.ppermute(head, axis, [((i + 1) % count, i) for i in range(ends)]),
            ],
            axis=dim,
        )
    return cells


def band_patches(extended, rows_out, flipped):
    padded = jnp.pad(extended, ((0, 0), (0, 0), (1, 1), (0, 0)))
    cols = extended.shape[2]
    pieces = []
    for first in range(3):
        for second in range(3):
            top = 2 - first if flipped else first
            left = 2 - second if flipped else second
            pieces.append(padded[:, top : top + rows_out, left : left + cols, :])
    return jnp.concatenate(pieces, axis=3).reshape(-1, 9 * extended.shape[3])


def causal_mix(act, weight):
    clips, frames, cells, chans = act.shape
    padded = jnp.pad(act, ((0, 0), (2, 0), (0, 0), (0, 0)))
    total = jnp.zeros((clips * frames * cells, chans), jnp.float32)
    for tap in range(3):
        earlier = padded[:, 2 - tap : 2 - tap + frames].reshape(-1, chans)
        total = total + jnp.dot(earlier, weight[tap], preferred_element_type=jnp.float32)
    return total.astype(jnp.bfloat16)


def anti_mix(cot, weight):
    clips, frames, cells, chans = cot.shape
    padded = jnp.pad(cot, ((0, 0), (0, 2), (0, 0), (0, 0)))
    total = jnp.zeros((clips * frames * cells, chans), jnp.float32)
    for tap in range(3):
        later = padded[:, tap : tap + frames].reshape(-1, chans)
        total = total + lax.dot_general(
            later, weight[tap], (((1,), (1,)), ((), ())), preferred_element_type=jnp.float32
        )
    return total.astype(jnp.bfloat16)


def tap_grads(act, cot):
    clips, frames, cells, chans = act.shape
    padded = jnp.pad(act, ((0, 0), (2, 0), (0, 0), (0, 0)))
    cot_flat = cot.reshape(-1, chans)
    parts = []
    for tap in range(3):
        earlier = padded[:, 2 - tap : 2 - tap + frames].reshape(-1, chans)
        parts.append(
            lax.dot_general(
                earlier, cot_flat, (((0,), (0,)), ((), ())), preferred_element_type=jnp.float32
            )
        )
    return jnp.stack(parts)


def silu_grad(act_grad, pre):
    sig = jax.nn.sigmoid(pre)
    return (act_grad.astype(jnp.float32) * sig * (1.0 + pre * (1.0 - sig))).astype(jnp.bfloat16)


def body(latents, cotangent, spatial_weight, temporal_weight):
    clips, frames, rows, cols, chans = latents.shape
    flat_w = spatial_weight.reshape(9 * chans, chans)
    flip_w = jnp.transpose(spatial_weight, (0, 1, 3, 2)).reshape(9 * chans, chans)
    cot_band = cotangent.reshape(clips, frames, rows * cols, chans)
    extended = with_halo(latents, (("tm", 2),), 1)
    patches = band_patches(extended.reshape(clips * frames, rows + 2, cols, chans), rows, False)
    pre = jnp.dot(patches, flat_w, preferred_element_type=jnp.float32)
    act = jax.nn.silu(pre).astype(jnp.bfloat16).reshape(clips, frames, rows * cols, chans)
    mixed = causal_mix(act, temporal_weight)
    act_grad = anti_mix(cot_band, temporal_weight)
    pre_grad = silu_grad(act_grad, pre)
    grad_ext = with_halo(pre_grad.reshape(clips, frames, rows, cols, chans), (("tm", 2),), 1)
    back = jnp.dot(
        band_patches(grad_ext.reshape(clips * frames, rows + 2, cols, chans), rows, True),
        flip_w,
        preferred_element_type=jnp.float32,
    )
    temporal_local = tap_grads(act, cot_band)
    block_out = (latents.reshape(-1, chans).astype(jnp.float32) + mixed.astype(jnp.float32)).astype(
        jnp.bfloat16
    )
    latents_grad = (cotangent.reshape(-1, chans).astype(jnp.float32) + back).astype(jnp.bfloat16)
    spatial_local = lax.dot_general(
        patches, pre_grad, (((0,), (0,)), ((), ())), preferred_element_type=jnp.float32
    )
    spatial_sum, temporal_sum = lax.psum((spatial_local, temporal_local), ("dp", "tm"))
    scale = (clips * lax.axis_size("dp") * frames * rows * lax.axis_size("tm") * cols) ** (-0.5)
    return (
        block_out.reshape(latents.shape),
        latents_grad.reshape(latents.shape),
        (spatial_sum * scale).reshape(3, 3, chans, chans),
        temporal_sum * scale,
    )


def solution(mesh):
    in_specs = (P("dp", None, "tm", None, None), P("dp", None, "tm", None, None), P(), P())
    out_specs = (P("dp", None, "tm", None, None), P("dp", None, "tm", None, None), P(), P())
    return jax.shard_map(body, mesh=mesh, in_specs=in_specs, out_specs=out_specs, check_vma=False)
```

profile of v0, /device:TPU:1, one launch (start us, length us, event | category | flops | bytes accessed | tf_op | source)
XLA Modules:
  0.0 337.2 jit_solution(11071545228273672446)
XLA Ops:
  7.2 2.4 fusion.37
  9.6 5.0 %collective-permute-start = (bf16[1,17,1,64,256]{4,3,2,1,0:T(8,128)(2,1)}, bf16[1,17,1,64,256]{4,3,2,1,0:T(8,128)(2,1)}, u32[]{:S(2)}, u32[]{:S(2)}) collective-permute-start(bf16[1,17,1,64,256]{4,3,2,1,0:T(8,128)(2,1)} %get-tuple-element.12), channel_id=1, source_target_pairs={{0,1},{1,2},{2,3},{3,4},{4,5},{5,6},{6,7},{7,8},{8,9},{9,10},{10,1... | collective-permute-start | bytes 1671176 | tf_op jit(solution)/shard_map/ppermute | solution.py:15
  14.6 1.3 collective-permute-start.1
  15.9 2.8 fusion.26
  18.7 1.5 copy.8
  20.2 0.2 pad_slice_fusion.12
  20.4 1.4 copy-done.3
  21.9 0.5 convolution_add_fusion.1
  22.4 3.0 collective-permute-done
  25.4 4.6 %collective-permute-done.1 = bf16[1,17,1,64,256]{4,3,2,1,0:T(8,128)(2,1)} collective-permute-done((bf16[1,17,1,64,256]{4,3,2,1,0:T(8,128)(2,1)}, bf16[1,17,1,64,256]{4,3,2,1,0:T(8,128)(2,1)}, u32[]{:S(2)}, u32[]{:S(2)}) %collective-permute-start.1) | collective-permute-done | bytes 557088 | tf_op jit(solution)/shard_map/ppermute | solution.py:17
  30.0 1.5 maximum_bitcast_fusion
  31.5 0.4 fusion.10
  31.9 0.1 slice_dynamic-update-slice_fusion.5
  32.0 0.6 fusion.11
  32.6 0.7 fusion.12
  33.4 0.6 fusion.13
  34.0 0.7 fusion.14
  34.7 0.1 slice_dynamic-update-slice_fusion.3
  34.8 0.6 fusion.15
  35.4 2.9 multiply_convert_fusion
  38.3 0.5 convolution_bitcast_fusion.2
  38.8 1.8 fusion.28
  40.6 1.0 fusion.9
  41.7 4.4 %fusion.38 = f32[2304,256]{1,0:T(8,128)} fusion(bf16[2176,2304]{1,0:T(8,128)(2,1)S(1)} %bitcast.83, bf16[2176,256]{1,0:T(8,128)(2,1)S(1)} %fusion.9), kind=kOutput, calls=%fused_computation.75 | convolution fusion | flops 2566914048 | bytes 13500416 | tf_op jit(solution)/shard_map/dot_general | solution.py:101
  46.1 1.2 fusion.36
  47.3 3.2 collective-permute-start.2
  50.6 1.3 collective-permute-start.3
  51.9 0.1 pad_slice_fusion.14
  52.0 0.5 convolution_bitcast_fusion
  52.5 0.5 convolution_bitcast_fusion.1
  53.1 0.9 pad_maximum_fusion
  54.0 2.5 convolution_add_fusion.3
  56.5 2.5 fusion.4
  59.0 1.2 collective-permute-done.2
  60.2 4.7 %collective-permute-done.3 = bf16[1,17,1,64,256]{4,3,2,1,0:T(8,128)(2,1)} collective-permute-done((bf16[1,17,1,64,256]{4,3,2,1,0:T(8,128)(2,1)}, bf16[1,17,1,64,256]{4,3,2,1,0:T(8,128)(2,1)}, u32[]{:S(2)}, u32[]{:S(2)}) %collective-permute-start.3) | collective-permute-done | bytes 557088 | tf_op jit(solution)/shard_map/ppermute | solution.py:17
  64.9 1.5 maximum_bitcast_fusion.1
  66.3 0.3 fusion.16
  66.7 0.1 slice_dynamic-update-slice_fusion.2
  66.8 0.7 fusion.17
  67.5 0.6 fusion.18
  68.2 0.7 fusion.19
  68.9 0.6 fusion.20
  69.6 0.7 fusion.21
  70.3 0.6 copy-done.7
  70.9 3.8 %fusion = bf16[2176,256]{1,0:T(8,128)(2,1)} fusion(bf16[2176,2304]{1,0:T(8,128)(2,1)S(1)} %bitcast.84, bf16[2304,256]{1,0:T(8,128)(2,1)S(1)} %bitcast.79, bf16[2176,256]{1,0:T(8,128)(2,1)S(1)} %bitcast.67), kind=kOutput, calls=%fused_computation.5 | convolution fusion | flops 2568585216 | bytes 13434880 | tf_op jit(solution)/shard_map/dot_general | solution.py:91
  74.6 251.4 %all-reduce.7.cloned.1.call-done = (f32[2304,256]{1,0:T(8,128)}, f32[3,256,256]{2,1,0:T(8,128)}) async-done(((f32[2304,256]{1,0:T(8,128)}, f32[3,256,256]{2,1,0:T(8,128)}), (f32[2304,256]{1,0:T(8,128)}, f32[3,256,256]{2,1,0:T(8,128)})) %all-reduce.7.cloned.1.call-update) | async-done | bytes 3145744 | tf_op jit(solution)/shard_map/psum | solution.py:104
  326.0 3.3 broadcast_multiply_fusion
  329.4 0.9 broadcast_multiply_fusion.1
  (23 shorter events, 0.4 us)
Async XLA Ops:
  7.2 8.7 %copy-start = (bf16[1,17,2,64,256]{4,3,2,1,0:T(8,128)(2,1)S(1)}, bf16[1,17,2,64,256]{4,3,2,1,0:T(8,128)(2,1)}, u32[]{:S(2)}) copy-start(bf16[1,17,2,64,256]{4,3,2,1,0:T(8,128)(2,1)} %param.5) | copy-start | bytes 3342340
  7.2 318.9 %all-reduce.7.cloned.1.call-start = ((), (), s32[]{:S(2)}) async-start(), calls=%async_computation | async-start | bytes 6291456 | tf_op jit(solution)/shard_map/psum | solution.py:104
  9.6 9.0 %copy-start.6 = (bf16[3,3,256,256]{3,2,1,0:T(8,128)(2,1)S(1)}, bf16[3,3,256,256]{3,2,1,0:T(8,128)(2,1)}, u32[]{:S(2)}) copy-start(bf16[3,3,256,256]{3,2,1,0:T(8,128)(2,1)} %param.6) | copy-start | bytes 3538948
  9.6 15.8 %collective-permute-start = (bf16[1,17,1,64,256]{4,3,2,1,0:T(8,128)(2,1)}, bf16[1,17,1,64,256]{4,3,2,1,0:T(8,128)(2,1)}, u32[]{:S(2)}, u32[]{:S(2)}) collective-permute-start(bf16[1,17,1,64,256]{4,3,2,1,0:T(8,128)(2,1)} %get-tuple-element.12), channel_id=1, source_target_pairs={{0,1},{1,2},{2,3},{3,4},{4,5},{5,6},{6,7},{7,8},{8,9},{9,10},{10,1... | collective-permute-start | bytes 1671176 | tf_op jit(solution)/shard_map/ppermute | solution.py:15
  14.6 15.4 %collective-permute-start.1 = (bf16[1,17,1,64,256]{4,3,2,1,0:T(8,128)(2,1)}, bf16[1,17,1,64,256]{4,3,2,1,0:T(8,128)(2,1)}, u32[]{:S(2)}, u32[]{:S(2)}) collective-permute-start(bf16[1,17,1,64,256]{4,3,2,1,0:T(8,128)(2,1)} %get-tuple-element.13), channel_id=1, source_target_pairs={{1,0},{2,1},{3,2},{4,3},{5,4},{6,5},{7,6},{8,7},{9,8},{10,9},{11,1... | collective-permute-start | bytes 1671176 | tf_op jit(solution)/shard_map/ppermute | solution.py:17
  20.2 1.6 copy-start.3
  20.2 1.7 copy-start.8
  21.9 8.2 %copy-start.1 = (bf16[1,17,2,64,256]{4,3,2,1,0:T(8,128)(2,1)S(1)}, bf16[1,17,2,64,256]{4,3,2,1,0:T(8,128)(2,1)}, u32[]{:S(2)}) copy-start(bf16[1,17,2,64,256]{4,3,2,1,0:T(8,128)(2,1)} %param.4) | copy-start | bytes 3342340
  41.7 4.4 %copy-start.4 = (bf16[2176,256]{1,0:T(8,128)(2,1)}, bf16[2176,256]{1,0:T(8,128)(2,1)S(1)}, u32[]{:S(2)}) copy-start(bf16[2176,256]{1,0:T(8,128)(2,1)S(1)} %fusion.9) | copy-start | bytes 3342340
  47.3 12.9 %collective-permute-start.2 = (bf16[1,17,1,64,256]{4,3,2,1,0:T(8,128)(2,1)}, bf16[1,17,1,64,256]{4,3,2,1,0:T(8,128)(2,1)}, u32[]{:S(2)}, u32[]{:S(2)}) collective-permute-start(bf16[1,17,1,64,256]{4,3,2,1,0:T(8,128)(2,1)} %get-tuple-element.6), channel_id=1, source_target_pairs={{0,1},{1,2},{2,3},{3,4},{4,5},{5,6},{6,7},{7,8},{8,9},{9,10},{10,1... | collective-permute-start | bytes 1671176 | tf_op jit(solution)/shard_map/ppermute | solution.py:15
  50.6 14.3 %collective-permute-start.3 = (bf16[1,17,1,64,256]{4,3,2,1,0:T(8,128)(2,1)}, bf16[1,17,1,64,256]{4,3,2,1,0:T(8,128)(2,1)}, u32[]{:S(2)}, u32[]{:S(2)}) collective-permute-start(bf16[1,17,1,64,256]{4,3,2,1,0:T(8,128)(2,1)} %get-tuple-element.7), channel_id=1, source_target_pairs={{1,0},{2,1},{3,2},{4,3},{5,4},{6,5},{7,6},{8,7},{9,8},{10,9},{11,1... | collective-permute-start | bytes 1671176 | tf_op jit(solution)/shard_map/ppermute | solution.py:17
  52.0 1.0 copy-start.2
  56.5 8.3 %copy-start.5 = (bf16[2176,256]{1,0:T(8,128)(2,1)S(1)}, bf16[2176,256]{1,0:T(8,128)(2,1)}, u32[]{:S(2)}) copy-start(bf16[2176,256]{1,0:T(8,128)(2,1)} %copy-done.4) | copy-start | bytes 3342340
  69.6 1.3 copy-start.7
  326.0 3.4 copy-start.9
Sparse Core Ops, SparseCore 0:
  54.1 271.8 all-reduce.6
where the time goes:
time: 338 us; the launch traced here: 337 us
  waiting for transfers between devices  265 us (78%)
  matrix products  23.6 us (7%)
  local copies, waits for them, and re-layouts  15.3 us (5%)
  between operations  14.3 us (4%)
  starting transfers between devices  10.8 us (3%)
  other arithmetic  8.16 us (2%)
    psum x1, waiting for transfers between devices, body(): lax.psum((spatial_local, temporal_local), ('dp', 'tm'))  251 us
    unnamed x37, local copies, waits for them, and re-layouts  10.1 us
    ppermute x2, waiting for transfers between devices, with_halo(): lax.ppermute(head, axis, [((i + 1) % count, i) for i in range(ends)])  9.29 us
    ppermute x2, starting transfers between devices, with_halo(): lax.ppermute(tail, axis, [(i, (i + 1) % count) for i in range(ends)])  8.21 us
    dot_general x3, matrix products, causal_mix(): jnp.dot(earlier, weight[tap], preferred_element_type=jnp.float32)  6.77 us
  transfers between devices with their start and end apart: 5, of which 5 were waited for; matrix products, arithmetic and copies ran while one was open for 6% of the time, Pallas kernels for 0%

commit v1 on v0

v1 whole, which is shorter than its diff:
```python
import jax
import jax.numpy as jnp
from jax import lax
from jax.experimental import pallas as pl
from jax.experimental.pallas import tpu as pltpu
from jax.sharding import PartitionSpec as P

F32 = jnp.float32
BF16 = jnp.bfloat16
NX, NY, NZ = 4, 4, 8
FRAMES, COLS, CH = 17, 64, 256
PAIRS = FRAMES // 2

CORE, XF, XB, XF2, ZS, YS, ZG, XG, CG, SLOTS = 0, 1, 2, 3, 4, 11, 14, 21, 24, 25


def peer(dp, tm):
    return (dp, tm)


def remote(src, dst, send, recv, device):
    return pltpu.make_async_remote_copy(
        src_ref=src, dst_ref=dst, send_sem=send, recv_sem=recv,
        device_id=device, device_id_type=pl.DeviceIdType.MESH,
    )


class Reduce:
    def __init__(self, here, grads, total, c_send, c_recv, x_send, x_recv, z_send, z_recv, y_buf, ssem, rsem):
        self.x, self.core, self.z, self.y = here
        self.grads, self.total = grads, total
        self.c_send, self.c_recv = c_send, c_recv
        self.x_send, self.x_recv = x_send, x_recv
        self.z_send, self.z_recv, self.y_buf = z_send, z_recv, y_buf
        self.ssem, self.rsem = ssem, rsem
        self.step = 1 - 2 * self.core
        self.copies = {}
        self.fwd = lax.rem(self.x + self.step + NX, NX)
        self.bwd = lax.rem(self.x - self.step + NX, NX)
        self.far = lax.rem(self.x + 2, NX)
        self.tm = self.z * NY + self.y

    def at_x(self, x):
        return peer(x * 2 + self.core, self.tm)

    def at_z(self, j):
        z = lax.rem(self.z + j, NZ)
        return z, peer(self.x * 2 + self.core, z * NY + self.y)

    def at_y(self, j):
        return peer(self.x * 2 + self.core, self.z * NY + lax.rem(self.y + j, NY))

    def partner(self):
        return peer(self.x * 2 + 1 - self.core, self.tm)

    def send(self, s, slot, src, dst, device):
        copy = remote(src, dst, self.ssem.at[s, slot], self.rsem.at[s, slot], device)
        copy.start()
        self.copies[s, slot] = copy

    def arrive(self, s, *slots):
        for slot in slots:
            self.copies[s, slot].wait_recv()

    def finish(self):
        for copy in self.copies.values():
            copy.wait_send()

    def tile(self, s):
        return self.core * 3 + s

    def stages(self, s):
        return self.x_first(s) if s < 2 else self.z_first(s)

    def core_out(self, s):
        other = (1 - self.core) * 3 + s
        self.c_send[s] = self.grads[other].astype(BF16)
        self.send(s, CORE, self.c_send.at[s], self.c_recv.at[s], self.partner())

    def core_back(self, s):
        t = self.tile(s)
        self.send(s, CG, self.total.at[t], self.total.at[t], self.partner())

    def y_out(self, s, value):
        self.y_buf[s, self.y] = value.astype(BF16)
        for j in range(1, NY):
            self.send(s, YS + j - 1, self.y_buf.at[s, self.y], self.y_buf.at[s, self.y], self.at_y(j))

    def y_sum(self, s):
        self.arrive(s, *range(YS, YS + NY - 1))
        value = self.y_buf[s, 0].astype(F32)
        for j in range(1, NY):
            value = value + self.y_buf[s, j].astype(F32)
        return value.astype(BF16)

    def x_first(self, s):
        t = self.tile(s)

        def local(x):
            return self.grads[t, x] + self.c_recv[s, x].astype(F32)

        def first():
            self.arrive(s, CORE)
            self.x_send[s, 0] = local(self.far).astype(BF16)
            self.send(s, XF, self.x_send.at[s, 0], self.x_recv.at[s, 0], self.at_x(self.fwd))
            self.x_send[s, 1] = local(self.bwd).astype(BF16)
            self.send(s, XB, self.x_send.at[s, 1], self.x_recv.at[s, 1], self.at_x(self.bwd))

        def second():
            self.arrive(s, XF)
            self.x_send[s, 2] = (local(self.fwd) + self.x_recv[s, 0].astype(F32)).astype(BF16)
            self.send(s, XF2, self.x_send.at[s, 2], self.x_recv.at[s, 2], self.at_x(self.fwd))

        def third():
            self.arrive(s, XB, XF2)
            own = local(self.x) + self.x_recv[s, 1].astype(F32) + self.x_recv[s, 2].astype(F32)
            self.grads[t, self.x] = own
            self.z_send[s, 0] = own.astype(BF16)
            for j in (4, 3, 5, 2, 6, 1, 7):
                z, device = self.at_z(j)
                self.send(s, ZS + j - 1, self.z_send.at[s, 0, z], self.z_recv.at[s, j - 1, 0], device)

        def fourth():
            self.arrive(s, *range(ZS, ZS + NZ - 1))
            own = self.grads[t, self.x, self.z]
            for j in range(NZ - 1):
                own = own + self.z_recv[s, j, 0].astype(F32)
            self.y_out(s, own)

        def fifth():
            self.total[t, self.x, self.z] = self.y_sum(s)
            block = self.total.at[t, self.x, self.z]
            for j in (4, 3, 5, 2, 6, 1, 7):
                self.send(s, ZG + j - 1, block, block, self.at_z(j)[1])

        def sixth():
            self.arrive(s, *range(ZG, ZG + NZ - 1))
            self.x_spread(s, lambda x: self.total.at[t, x])

        def seventh():
            self.x_forward(s, lambda x: self.total.at[t, x])

        def eighth():
            self.arrive(s, XG + 1, XG + 2)
            self.core_back(s)

        return [lambda: self.core_out(s), first, second, third, fourth, fifth, sixth, seventh, eighth, lambda: self.arrive(s, CG)]

    def x_spread(self, s, block):
        mine = block(self.x)
        self.send(s, XG, mine, mine, self.at_x(self.fwd))
        self.send(s, XG + 1, mine, mine, self.at_x(self.bwd))

    def x_forward(self, s, block):
        self.arrive(s, XG)
        got = block(self.bwd)
        self.send(s, XG + 2, got, got, self.at_x(self.fwd))

    def z_first(self, s):
        t = self.tile(s)

        def chunk(z):
            return z // 2, pl.ds(lax.rem(z, 2) * NX, NX)

        def cell(x):
            return self.z // 2, lax.rem(self.z, 2) * NX + x

        def first():
            self.arrive(s, CORE)
            self.z_send[s] = (self.grads[t] + self.c_recv[s].astype(F32)).astype(BF16)
            for j in (4, 3, 5, 2, 6, 1, 7):
                z, device = self.at_z(j)
                self.send(s, ZS + j - 1, self.z_send.at[(s, *chunk(z))], self.z_recv.at[s, j - 1], device)

        def second():
            self.arrive(s, *range(ZS, ZS + NZ - 1))
            where = chunk(self.z)
            own = self.grads[(t, *where)] + self.c_recv[(s, *where)].astype(F32)
            for j in range(NZ - 1):
                own = own + self.z_recv[s, j].astype(F32)
            self.grads[(t, *where)] = own
            self.x_send[s, 0, 0] = self.grads[(t, *cell(self.far))].astype(BF16)
            self.send(s, XF, self.x_send.at[s, 0, 0], self.x_recv.at[s, 0, 0], self.at_x(self.fwd))
            self.x_send[s, 1, 0] = self.grads[(t, *cell(self.bwd))].astype(BF16)
            self.send(s, XB, self.x_send.at[s, 1, 0], self.x_recv.at[s, 1, 0], self.at_x(self.bwd))

        def third():
            self.arrive(s, XF)
            self.x_send[s, 2, 0] = (self.grads[(t, *cell(self.fwd))] + self.x_recv[s, 0, 0].astype(F32)).astype(BF16)
            self.send(s, XF2, self.x_send.at[s, 2, 0], self.x_recv.at[s, 2, 0], self.at_x(self.fwd))

        def fourth():
            self.arrive(s, XB, XF2)
            own = self.grads[(t, *cell(self.x))] + self.x_recv[s, 1, 0].astype(F32) + self.x_recv[s, 2, 0].astype(F32)
            self.y_out(s, own)

        def fifth():
            self.total[(t, *cell(self.x))] = self.y_sum(s)
            self.x_spread(s, lambda x: self.total.at[(t, *cell(x))])

        def sixth():
            self.x_forward(s, lambda x: self.total.at[(t, *cell(x))])

        def seventh():
            self.arrive(s, XG + 1, XG + 2)
            block = self.total.at[(t, *chunk(self.z))]
            for j in (4, 3, 5, 2, 6, 1, 7):
                self.send(s, ZG + j - 1, block, block, self.at_z(j)[1])

        def eighth():
            self.arrive(s, *range(ZG, ZG + NZ - 1))
            self.core_back(s)

        return [lambda: self.core_out(s), first, second, third, fourth, fifth, sixth, seventh, eighth, lambda: self.arrive(s, CG)]


REDUCE_SCRATCH = [
    pltpu.VMEM((6, 4, 8, 32, 128), F32),
    pltpu.VMEM((6, 4, 8, 32, 128), BF16),
    pltpu.VMEM((3, 4, 8, 32, 128), BF16),
    pltpu.VMEM((3, 4, 8, 32, 128), BF16),
    pltpu.VMEM((3, 3, 8, 32, 128), BF16),
    pltpu.VMEM((3, 3, 8, 32, 128), BF16),
    pltpu.VMEM((3, 4, 8, 32, 128), BF16),
    pltpu.VMEM((3, 7, 4, 32, 128), BF16),
    pltpu.VMEM((3, 4, 32, 128), BF16),
    pltpu.SemaphoreType.DMA((3, SLOTS)),
    pltpu.SemaphoreType.DMA((3, SLOTS)),
]


def position():
    dp, tm = lax.axis_index("dp"), lax.axis_index("tm")
    return dp // 2, lax.rem(dp, 2), tm // NY, lax.rem(tm, NY)


def greet(x, core, z, y, extra=()):
    barrier = pltpu.get_barrier_semaphore()
    tm = z * NY + y
    peers = [peer(x * 2 + 1 - core, tm)]
    peers += [peer(lax.rem(x + j, NX) * 2 + core, tm) for j in (1, NX - 1)]
    peers += [peer(x * 2 + core, z * NY + lax.rem(y + j, NY)) for j in range(1, NY)]
    peers += [peer(x * 2 + core, lax.rem(z + j, NZ) * NY + y) for j in range(1, NZ)]
    peers += list(extra)
    for device in peers:
        pl.semaphore_signal(barrier, inc=1, device_id=device, device_id_type=pl.DeviceIdType.MESH)
    return barrier, len(peers)


NT = (((1,), (1,)), ((), ()))
TN = (((0,), (0,)), ((), ()))


def dot(a, b, dims=(((1,), (0,)), ((), ()))):
    return lax.dot_general(a, b, dims, preferred_element_type=F32)


def shifted(value, up):
    cells = value.shape[0]
    col = lax.rem(lax.broadcasted_iota(jnp.int32, value.shape, 0), COLS)
    if up:
        return jnp.where(col == 0, 0.0, pltpu.roll(value, 1, 0))
    return jnp.where(col == COLS - 1, 0.0, pltpu.roll(value, cells - 1, 0))


def kernel(
    lat, cot, weight, mix, block_out, lat_grad, grad_out,
    ext, cotx, actx, agrad, pg3, pgh, w_v, mix_v, out_b, out_g,
    grads, total, c_send, c_recv, x_send, x_recv, z_send, z_recv, y_buf, ssem, rsem,
    load_sem, halo_s, halo_r, back_s, back_r, store_sem,
):
    here = position()
    x, core, z, y = here
    dp, tm = x * 2 + core, z * NY + y
    bands = NZ * NY
    below = peer(dp, lax.rem(tm + 1, bands))
    above = peer(dp, lax.rem(tm + bands - 1, bands))
    barrier, count = greet(x, core, z, y, (above, below))

    loads = [
        pltpu.make_async_copy(cot, cotx.at[pl.ds(0, FRAMES)], load_sem.at[0]),
        pltpu.make_async_copy(mix, mix_v, load_sem.at[1]),
        pltpu.make_async_copy(lat, ext.at[:, pl.ds(1, 2)], load_sem.at[2]),
    ]
    for a in range(3):
        for b in range(3):
            loads.append(pltpu.make_async_copy(weight.at[a, b], w_v.at[a, :, pl.ds(b * CH, CH)], load_sem.at[3 + a * 3 + b]))
    for load in loads:
        load.start()
    cotx[FRAMES:] = jnp.zeros((2, 2 * COLS, CH), BF16)
    actx[:2] = jnp.zeros((2, 2 * COLS, CH), BF16)
    pl.semaphore_wait(barrier, count)

    def halo(i, first, size):
        frames = pl.ds(first, size)
        return (
            remote(lat.at[frames, 1], ext.at[frames, 0], halo_s.at[0, i], halo_r.at[0, i], below),
            remote(lat.at[frames, 0], ext.at[frames, 3], halo_s.at[1, i], halo_r.at[1, i], above),
        )

    def grad_halo(i, first, size):
        frames = pl.ds(first, size)
        return (
            remote(pg3.at[frames, 2, :, pl.ds(CH, CH)], pgh.at[0, frames], back_s.at[0, i], back_r.at[0, i], below),
            remote(pg3.at[frames, 1, :, pl.ds(CH, CH)], pgh.at[1, frames], back_s.at[1, i], back_r.at[1, i], above),
        )

    def over(make, act):
        @pl.loop(0, PAIRS)
        def _(i):
            for copy in make(i, 2 * i, 2):
                act(copy)
        for copy in make(PAIRS, FRAMES - 1, 1):
            act(copy)

    over(halo, lambda copy: copy.start())

    loads[0].wait()
    loads[1].wait()

    @pl.loop(0, 3)
    def _(i):
        first = jnp.minimum(6 * i, FRAMES - 6)
        value = jnp.zeros((6 * 2 * COLS, CH), F32)
        for k in range(3):
            value = value + dot(cotx[pl.ds(first + k, 6)].reshape(-1, CH), mix_v[k], NT)
        agrad[pl.ds(first, 6)] = value.astype(BF16).reshape(6, 2 * COLS, CH)

    for load in loads[2:]:
        load.wait()

    grads[...] = jnp.zeros_like(grads)

    def add_grad(index, value):
        for t in range(6):
            grads[t, index] += value[:, t * 128 : (t + 1) * 128].reshape(8, 32, 128)

    def chunk(i, first, size):
        for copy in halo(i, first, size):
            copy.wait_recv()
        frames = pl.ds(first, size)
        cells = size * 2 * COLS

        @pl.when(tm == 0)
        def _():
            ext[frames, 0] = jnp.zeros((size, COLS, CH), BF16)

        @pl.when(tm == bands - 1)
        def _():
            ext[frames, 3] = jnp.zeros((size, COLS, CH), BF16)

        parts = jnp.zeros((cells, 3 * CH), F32)
        for a in range(3):
            parts = parts + dot(ext[frames, a : a + 2].reshape(cells, CH), w_v[a])
        pre = shifted(parts[:, :CH], True) + parts[:, CH : 2 * CH] + shifted(parts[:, 2 * CH :], False)
        sig = jax.nn.sigmoid(pre)
        act = (pre * sig).astype(BF16)
        actx[pl.ds(first + 2, size)] = act.reshape(size, 2 * COLS, CH)
        ag = agrad[frames].reshape(cells, CH).astype(F32)
        pg = ag * sig * (1.0 + pre * (1.0 - sig))
        three = jnp.concatenate([shifted(pg, False), pg, shifted(pg, True)], axis=1).astype(BF16)
        pg3[frames, 1:3] = three.reshape(size, 2, COLS, 3 * CH)
        for a in range(3):
            add_grad(a, dot(ext[frames, a : a + 2].reshape(cells, CH), three, TN))
        cots = jnp.concatenate([cotx[pl.ds(first + k, size)].reshape(cells, CH) for k in range(3)], axis=1)
        add_grad(3, dot(act, cots, TN))

    @pl.loop(0, PAIRS)
    def _(i):
        chunk(i, 2 * i, 2)

    chunk(PAIRS, FRAMES - 1, 1)
    over(grad_halo, lambda copy: copy.start())

    def mix_unit(i, first, size):
        frames = pl.ds(first, size)
        value = jnp.zeros((size * 2 * COLS, CH), F32)
        for k in range(3):
            value = value + dot(actx[pl.ds(first + 2 - k, size)].reshape(-1, CH), mix_v[k])
        value = value.astype(BF16).astype(F32) + ext[frames, 1:3].reshape(-1, CH).astype(F32)
        out_b[frames] = value.astype(BF16).reshape(size, 2 * COLS, CH)
        pltpu.make_async_copy(out_b.at[frames], block_out.at[frames], store_sem.at[0, i]).start()

    def back_unit(i, first, size):
        frames = pl.ds(first, size)
        cells = size * 2 * COLS
        for copy in grad_halo(i, first, size):
            copy.wait_recv()
        for side, row, edge in ((0, 0, 0), (1, 3, bands - 1)):
            value = pgh[side, frames].reshape(size * COLS, CH).astype(F32)
            value = jnp.where(tm == edge, 0.0, value)
            three = jnp.concatenate([shifted(value, False), value, shifted(value, True)], axis=1)
            pg3[frames, row] = three.astype(BF16).reshape(size, COLS, 3 * CH)
        value = cotx[frames].reshape(cells, CH).astype(F32)
        back = jnp.zeros((cells, CH), F32)
        for a in range(3):
            back = back + dot(pg3[frames, 2 - a : 4 - a].reshape(cells, 3 * CH), w_v[a], NT)
        out_g[frames] = (value + back).astype(BF16).reshape(size, 2 * COLS, CH)
        pltpu.make_async_copy(out_g.at[frames], lat_grad.at[frames], store_sem.at[1, i]).start()

    def units(unit, low, high):
        if low < min(high, PAIRS):
            @pl.loop(low, min(high, PAIRS))
            def _(i):
                unit(i, 2 * i, 2)
        if high > PAIRS:
            unit(PAIRS, FRAMES - 1, 1)

    reduce = Reduce(here, grads, total, c_send, c_recv, x_send, x_recv, z_send, z_recv, y_buf, ssem, rsem)
    steps = [reduce.stages(s) for s in range(3)]
    filler = {0: (mix_unit, 0, 3), 1: (mix_unit, 3, 9), 2: (back_unit, 0, 2), 3: (back_unit, 2, 5), 4: (back_unit, 5, 7), 5: (back_unit, 7, 9)}
    for stage in range(10):
        for s in (2, 0, 1):
            steps[s][stage]()
        if stage in filler:
            units(*filler[stage])

    outs = []
    for t in range(6):
        b, half = t // 2, t % 2
        out = pltpu.make_async_copy(total.at[t], grad_out.at[:, b, :, :, pl.ds(half * 128, 128)], load_sem.at[t])
        out.start()
        outs.append(out)
    reduce.finish()
    over(halo, lambda copy: copy.wait_send())
    over(grad_halo, lambda copy: copy.wait_send())

    def stores(i, first, size):
        frames = pl.ds(first, size)
        return (
            pltpu.make_async_copy(out_b.at[frames], block_out.at[frames], store_sem.at[0, i]),
            pltpu.make_async_copy(out_g.at[frames], lat_grad.at[frames], store_sem.at[1, i]),
        )

    over(stores, lambda copy: copy.wait())
    for out in outs:
        out.wait()


def body(latents, cotangent, spatial_weight, temporal_weight):
    clips, frames, rows, cols, chans = latents.shape
    cells = rows * cols
    any_spec = pl.BlockSpec(memory_space=pl.ANY)
    half = jax.ShapeDtypeStruct((frames, cells, chans), BF16)
    block_out, lat_grad, grad = pl.pallas_call(
        kernel,
        out_shape=(half, half, jax.ShapeDtypeStruct((4, 3, 8, 32, 256), BF16)),
        in_specs=[any_spec] * 4,
        out_specs=(any_spec,) * 3,
        scratch_shapes=[
            pltpu.VMEM((frames, 4, cols, chans), BF16),
            pltpu.VMEM((frames + 2, cells, chans), BF16),
            pltpu.VMEM((frames + 2, cells, chans), BF16),
            pltpu.VMEM((frames, cells, chans), BF16),
            pltpu.VMEM((frames, 4, cols, 3 * chans), BF16),
            pltpu.VMEM((2, frames, cols, chans), BF16),
            pltpu.VMEM((3, chans, 3 * chans), BF16),
            pltpu.VMEM((3, chans, chans), BF16),
            pltpu.VMEM((frames, cells, chans), BF16),
            pltpu.VMEM((frames, cells, chans), BF16),
            *REDUCE_SCRATCH,
            pltpu.SemaphoreType.DMA((12,)),
            pltpu.SemaphoreType.DMA((2, PAIRS + 1)),
            pltpu.SemaphoreType.DMA((2, PAIRS + 1)),
            pltpu.SemaphoreType.DMA((2, PAIRS + 1)),
            pltpu.SemaphoreType.DMA((2, PAIRS + 1)),
            pltpu.SemaphoreType.DMA((2, PAIRS + 1)),
        ],
        compiler_params=pltpu.CompilerParams(
            collective_id=0, has_side_effects=True, vmem_limit_bytes=60 * 1024 * 1024
        ),
    )(
        latents.reshape(frames, rows, cols, chans),
        cotangent.reshape(frames, cells, chans),
        spatial_weight,
        temporal_weight,
    )
    scale = (clips * lax.axis_size("dp") * frames * rows * lax.axis_size("tm") * cols) ** (-0.5)
    grad = grad.reshape(4, 3, chans, chans)
    return (
        block_out.reshape(latents.shape),
        lat_grad.reshape(latents.shape),
        grad[:3].astype(F32) * scale,
        grad[3].astype(F32) * scale,
    )


def solution(mesh):
    in_specs = (P("dp", None, "tm", None, None), P("dp", None, "tm", None, None), P(), P())
    return jax.shard_map(body, mesh=mesh, in_specs=in_specs, out_specs=in_specs, check_vma=False)
```

time: 338 us -> 84.9 us (0.25)
  waiting for transfers between devices: 265 us -> 0 us
  Pallas kernels: 0 us -> 76.4 us
  matrix products: 23.6 us -> 0 us
  between operations: 14.3 us -> 0.64 us
  local copies, waits for them, and re-layouts: 15.3 us -> 2.64 us
  starting transfers between devices: 10.8 us -> 0 us
    psum x1 -> x0, waiting for transfers between devices: 251 us -> none  [body(): lax.psum((spatial_local, temporal_local), ('dp', 'tm'))]
    pallas_call x0 -> x1, Pallas kernels: none -> 76.4 us  [body(): pl.pallas_call(kernel, out_shape=(half, half, jax.ShapeDtypeStruct((4, 3,...]
    dot_general x12 -> x0, matrix products: 23.6 us -> none  [the longest x3 6.77 us: causal_mix(): jnp.dot(earlier, weight[tap], preferred_element_type=jnp.float32)]
    ppermute x4 -> x0, waiting for transfers between devices: 13.5 us -> none  [the longest x2 9.29 us: with_halo(): lax.ppermute(head, axis, [((i + 1) % count, i) for i in range(ends)])]
    ppermute x4 -> x0, starting transfers between devices: 10.8 us -> none  [the longest x2 8.21 us: with_halo(): lax.ppermute(tail, axis, [(i, (i + 1) % count) for i in range(ends)])]
    unnamed x37 -> x6, local copies, waits for them, and re-layouts: 10.1 us -> 2.64 us
    slice x4 -> x0, local copies, waits for them, and re-layouts: 3.99 us -> none  [the longest x2 3.67 us: with_halo(): lax.slice_in_dim(cells, cells.shape[dim] - width, cells.shape[dim], axis=...]
  transfers between devices with their start and end apart: 5 -> 0, of which waited for: 5 -> 0; matrix products, arithmetic and copies ran while one was open for 6% -> 0% of each run, Pallas kernels for 0% -> 0%
where the time goes in v1:
time: 84.9 us; the launch traced here: 84.7 us
  Pallas kernels  76.4 us (90%)
  other arithmetic  5.07 us (6%)
  local copies, waits for them, and re-layouts  2.64 us (3%)
    pallas_call x1, Pallas kernels, body(): pl.pallas_call(kernel, out_shape=(half, half, jax.ShapeDtypeStruct((4, 3,...  76.4 us
    mul x1, other arithmetic, body(): grad[:3].astype(F32) * scale  3.1 us
    unnamed x6, local copies, waits for them, and re-layouts  2.64 us
    mul x1, other arithmetic, body(): grad[3].astype(F32) * scale  1.97 us

profile of v1, /device:TPU:1, one launch (start us, length us, event | category | flops | bytes accessed | tf_op | source)
XLA Modules:
  0.0 84.7 jit_solution(15522075308359619514)
XLA Ops:
  0.6 76.4 %shard_map.75 = (bf16[17,128,256]{2,1,0:T(8,128)(2,1)}, bf16[17,128,256]{2,1,0:T(8,128)(2,1)}, bf16[4,3,8,32,256]{4,3,2,1,0:T(8,128)(2,1)}) custom-call(bf16[17,2,64,256]{3,2,1,0:T(8,128)(2,1)} %bitcast.7, bf16[17,128,256]{2,1,0:T(8,128)(2,1)} %bitcast.8, bf16[3,3,256,256]{3,2,1,0:T(8,128)(2,1)} %weight.1, bf16[3,256,256]{2,1,0:T(8,128)(2,1)} %mix.1), custom_call_target="tpu_custom_call" | custom-call | tf_op jit(solution)/shard_map/pallas_call | solution.py:445
  77.0 2.0 %convert_multiply_fusion.1 = f32[1,3,8,32,256]{4,3,2,1,0:T(8,128)} fusion(bf16[4,3,8,32,256]{4,3,2,1,0:T(8,128)(2,1)} %get-tuple-element.9), kind=kLoop, calls=%fused_computation.1 | loop fusion | flops 393216 | bytes 1179648 | tf_op jit(solution)/shard_map/mul | solution.py:484
  79.0 0.0 copy-start.1
  79.0 3.1 %convert_multiply_fusion = f32[3,3,8,32,256]{4,3,2,1,0:T(8,128)} fusion(bf16[4,3,8,32,256]{4,3,2,1,0:T(8,128)(2,1)} %get-tuple-element.9), kind=kLoop, calls=%fused_computation | loop fusion | flops 1179648 | bytes 3538944 | tf_op jit(solution)/shard_map/mul | solution.py:483
  82.1 0.0 copy-start
  82.1 0.0 copy-done.1
  82.1 1.0 %copy.10 = bf16[1,17,2,64,256]{4,3,2,1,0:T(8,128)(2,1)} copy(bf16[1,17,2,64,256]{4,3,2,1,0:T(8,128)(2,1)S(1)} %bitcast.10) | data formatting | bytes 2228224
  83.1 0.7 copy-done
  83.8 1.0 %copy.11 = bf16[1,17,2,64,256]{4,3,2,1,0:T(8,128)(2,1)} copy(bf16[1,17,2,64,256]{4,3,2,1,0:T(8,128)(2,1)S(1)} %bitcast.9) | data formatting | bytes 2228224
Async XLA Ops:
  79.0 3.1 %copy-start.1 = (bf16[17,128,256]{2,1,0:T(8,128)(2,1)S(1)}, bf16[17,128,256]{2,1,0:T(8,128)(2,1)}, u32[]{:S(2)}) copy-start(bf16[17,128,256]{2,1,0:T(8,128)(2,1)} %get-tuple-element.7) | copy-start | bytes 3342340
  82.1 1.6 %copy-start = (bf16[17,128,256]{2,1,0:T(8,128)(2,1)S(1)}, bf16[17,128,256]{2,1,0:T(8,128)(2,1)}, u32[]{:S(2)}) copy-start(bf16[17,128,256]{2,1,0:T(8,128)(2,1)} %get-tuple-element.8) | copy-start | bytes 3342340

commit v2 on v1

--- a/solution.py
+++ b/solution.py
@@ -1,3 +1,5 @@
+import functools
+
 import jax
 import jax.numpy as jnp
 from jax import lax
@@ -9,6 +11,7 @@
 BF16 = jnp.bfloat16
 NX, NY, NZ = 4, 4, 8
 FRAMES, COLS, CH = 17, 64, 256
+VMEM_LIMIT = 56 * 1024 * 1024
 PAIRS = FRAMES // 2
 
 CORE, XF, XB, XF2, ZS, YS, ZG, XG, CG, SLOTS = 0, 1, 2, 3, 4, 11, 14, 21, 24, 25
@@ -70,7 +73,7 @@
         return self.core * 3 + s
 
     def stages(self, s):
-        return self.x_first(s) if s < 2 else self.z_first(s)
+        return self.x_first(s)
 
     def core_out(self, s):
         other = (1 - self.core) * 3 + s
@@ -156,67 +159,9 @@
         got = block(self.bwd)
         self.send(s, XG + 2, got, got, self.at_x(self.fwd))
 
-    def z_first(self, s):
-        t = self.tile(s)
-
-        def chunk(z):
-            return z // 2, pl.ds(lax.rem(z, 2) * NX, NX)
-
-        def cell(x):
-            return self.z // 2, lax.rem(self.z, 2) * NX + x
-
-        def first():
-            self.arrive(s, CORE)
-            self.z_send[s] = (self.grads[t] + self.c_recv[s].astype(F32)).astype(BF16)
-            for j in (4, 3, 5, 2, 6, 1, 7):
-                z, device = self.at_z(j)
-                self.send(s, ZS + j - 1, self.z_send.at[(s, *chunk(z))], self.z_recv.at[s, j - 1], device)
-
-        def second():
-            self.arrive(s, *range(ZS, ZS + NZ - 1))
-            where = chunk(self.z)
-            own = self.grads[(t, *where)] + self.c_recv[(s, *where)].astype(F32)
-            for j in range(NZ - 1):
-                own = own + self.z_recv[s, j].astype(F32)
-            self.grads[(t, *where)] = own
-            self.x_send[s, 0, 0] = self.grads[(t, *cell(self.far))].astype(BF16)
-            self.send(s, XF, self.x_send.at[s, 0, 0], self.x_recv.at[s, 0, 0], self.at_x(self.fwd))
-            self.x_send[s, 1, 0] = self.grads[(t, *cell(self.bwd))].astype(BF16)
-            self.send(s, XB, self.x_send.at[s, 1, 0], self.x_recv.at[s, 1, 0], self.at_x(self.bwd))
-
-        def third():
-            self.arrive(s, XF)
-            self.x_send[s, 2, 0] = (self.grads[(t, *cell(self.fwd))] + self.x_recv[s, 0, 0].astype(F32)).astype(BF16)
-            self.send(s, XF2, self.x_send.at[s, 2, 0], self.x_recv.at[s, 2, 0], self.at_x(self.fwd))
-
-        def fourth():
-            self.arrive(s, XB, XF2)
-            own = self.grads[(t, *cell(self.x))] + self.x_recv[s, 1, 0].astype(F32) + self.x_recv[s, 2, 0].astype(F32)
-            self.y_out(s, own)
-
-        def fifth():
-            self.total[(t, *cell(self.x))] = self.y_sum(s)
-            self.x_spread(s, lambda x: self.total.at[(t, *cell(x))])
-
-        def sixth():
-            self.x_forward(s, lambda x: self.total.at[(t, *cell(x))])
-
-        def seventh():
-            self.arrive(s, XG + 1, XG + 2)
-            block = self.total.at[(t, *chunk(self.z))]
-            for j in (4, 3, 5, 2, 6, 1, 7):
-                self.send(s, ZG + j - 1, block, block, self.at_z(j)[1])
-
-        def eighth():
-            self.arrive(s, *range(ZG, ZG + NZ - 1))
-            self.core_back(s)
-
-        return [lambda: self.core_out(s), first, second, third, fourth, fifth, sixth, seventh, eighth, lambda: self.arrive(s, CG)]
-
 
 REDUCE_SCRATCH = [
     pltpu.VMEM((6, 4, 8, 32, 128), F32),
-    pltpu.VMEM((6, 4, 8, 32, 128), BF16),
     pltpu.VMEM((3, 4, 8, 32, 128), BF16),
     pltpu.VMEM((3, 4, 8, 32, 128), BF16),
     pltpu.VMEM((3, 3, 8, 32, 128), BF16),
@@ -264,10 +209,10 @@
 
 
 def kernel(
-    lat, cot, weight, mix, block_out, lat_grad, grad_out,
-    ext, cotx, actx, agrad, pg3, pgh, w_v, mix_v, out_b, out_g,
-    grads, total, c_send, c_recv, x_send, x_recv, z_send, z_recv, y_buf, ssem, rsem,
-    load_sem, halo_s, halo_r, back_s, back_r, store_sem,
+    lat, cot, weight, mix, out_b, out_g, total,
+    ext, cotx, actx, agrad, pg3, pgh, w_v, mix_v,
+    grads, c_send, c_recv, x_send, x_recv, z_send, z_recv, y_buf, ssem, rsem,
+    load_sem, halo_s, halo_r, back_s, back_r,
 ):
     here = position()
     x, core, z, y = here
@@ -370,7 +315,17 @@
         chunk(i, 2 * i, 2)
 
     chunk(PAIRS, FRAMES - 1, 1)
-    over(grad_halo, lambda copy: copy.start())
+    def issue(low, high):
+        if low < min(high, PAIRS):
+            @pl.loop(low, min(high, PAIRS))
+            def _(i):
+                for copy in grad_halo(i, 2 * i, 2):
+                    copy.start()
+        if high > PAIRS:
+            for copy in grad_halo(PAIRS, FRAMES - 1, 1):
+                copy.start()
+
+    issue(0, 5)
 
     def mix_unit(i, first, size):
         frames = pl.ds(first, size)
@@ -379,7 +334,6 @@
             value = value + dot(actx[pl.ds(first + 2 - k, size)].reshape(-1, CH), mix_v[k])
         value = value.astype(BF16).astype(F32) + ext[frames, 1:3].reshape(-1, CH).astype(F32)
         out_b[frames] = value.astype(BF16).reshape(size, 2 * COLS, CH)
-        pltpu.make_async_copy(out_b.at[frames], block_out.at[frames], store_sem.at[0, i]).start()
 
     def back_unit(i, first, size):
         frames = pl.ds(first, size)
@@ -396,7 +350,6 @@
         for a in range(3):
             back = back + dot(pg3[frames, 2 - a : 4 - a].reshape(cells, 3 * CH), w_v[a], NT)
         out_g[frames] = (value + back).astype(BF16).reshape(size, 2 * COLS, CH)
-        pltpu.make_async_copy(out_g.at[frames], lat_grad.at[frames], store_sem.at[1, i]).start()
 
     def units(unit, low, high):
         if low < min(high, PAIRS):
@@ -408,45 +361,45 @@
 
     reduce = Reduce(here, grads, total, c_send, c_recv, x_send, x_recv, z_send, z_recv, y_buf, ssem, rsem)
     steps = [reduce.stages(s) for s in range(3)]
-    filler = {0: (mix_unit, 0, 3), 1: (mix_unit, 3, 9), 2: (back_unit, 0, 2), 3: (back_unit, 2, 5), 4: (back_unit, 5, 7), 5: (back_unit, 7, 9)}
+    filler = {0: (mix_unit, 0, 3), 1: (mix_unit, 3, 9), 3: (back_unit, 0, 3), 5: (back_unit, 3, 5), 7: (back_unit, 5, 7), 8: (back_unit, 7, 9)}
     for stage in range(10):
-        for s in (2, 0, 1):
+        for s in range(3):
             steps[s][stage]()
+        if stage == 5:
+            issue(5, 9)
         if stage in filler:
             units(*filler[stage])
 
-    outs = []
-    for t in range(6):
-        b, half = t // 2, t % 2
-        out = pltpu.make_async_copy(total.at[t], grad_out.at[:, b, :, :, pl.ds(half * 128, 128)], load_sem.at[t])
-        out.start()
-        outs.append(out)
     reduce.finish()
     over(halo, lambda copy: copy.wait_send())
     over(grad_halo, lambda copy: copy.wait_send())
 
-    def stores(i, first, size):
-        frames = pl.ds(first, size)
-        return (
-            pltpu.make_async_copy(out_b.at[frames], block_out.at[frames], store_sem.at[0, i]),
-            pltpu.make_async_copy(out_g.at[frames], lat_grad.at[frames], store_sem.at[1, i]),
-        )
-
-    over(stores, lambda copy: copy.wait())
-    for out in outs:
-        out.wait()
+
+def tail_kernel(scale, mixed, back, total, block_out, lat_grad, spatial, temporal, wide, sem):
+    copies = [pltpu.make_async_copy(mixed, block_out, sem.at[0]), pltpu.make_async_copy(back, lat_grad, sem.at[1])]
+    for copy in copies:
+        copy.start()
+    for a in range(4):
+        for t in range(6):
+            wide[a, t // 2, :, :, (t % 2) * 128 : (t % 2) * 128 + 128] = total[t, a].astype(F32) * scale
+        out = pltpu.make_async_copy(wide.at[a], spatial.at[a] if a < 3 else temporal, sem.at[2 + a])
+        out.start()
+        copies.append(out)
+    for copy in copies:
+        copy.wait()
 
 
 def body(latents, cotangent, spatial_weight, temporal_weight):
     clips, frames, rows, cols, chans = latents.shape
     cells = rows * cols
     any_spec = pl.BlockSpec(memory_space=pl.ANY)
-    half = jax.ShapeDtypeStruct((frames, cells, chans), BF16)
-    block_out, lat_grad, grad = pl.pallas_call(
+    vmem_spec = pl.BlockSpec(memory_space=pltpu.VMEM)
+    half = pltpu.VMEM((frames, cells, chans), BF16)
+    results = pl.pallas_call(
         kernel,
-        out_shape=(half, half, jax.ShapeDtypeStruct((4, 3, 8, 32, 256), BF16)),
+        out_shape=(half, half, pltpu.VMEM((6, 4, 8, 32, 128), BF16)),
         in_specs=[any_spec] * 4,
-        out_specs=(any_spec,) * 3,
+        out_specs=(vmem_spec,) * 3,
         scratch_shapes=[
             pltpu.VMEM((frames, 4, cols, chans), BF16),
             pltpu.VMEM((frames + 2, cells, chans), BF16),
@@ -456,18 +409,15 @@
             pltpu.VMEM((2, frames, cols, chans), BF16),
             pltpu.VMEM((3, chans, 3 * chans), BF16),
             pltpu.VMEM((3, chans, chans), BF16),
-            pltpu.VMEM((frames, cells, chans), BF16),
-            pltpu.VMEM((frames, cells, chans), BF16),
             *REDUCE_SCRATCH,
             pltpu.SemaphoreType.DMA((12,)),
             pltpu.SemaphoreType.DMA((2, PAIRS + 1)),
             pltpu.SemaphoreType.DMA((2, PAIRS + 1)),
             pltpu.SemaphoreType.DMA((2, PAIRS + 1)),
             pltpu.SemaphoreType.DMA((2, PAIRS + 1)),
-            pltpu.SemaphoreType.DMA((2, PAIRS + 1)),
         ],
         compiler_params=pltpu.CompilerParams(
-            collective_id=0, has_side_effects=True, vmem_limit_bytes=60 * 1024 * 1024
+            collective_id=0, has_side_effects=True, vmem_limit_bytes=VMEM_LIMIT
         ),
     )(
         latents.reshape(frames, rows, cols, chans),
@@ -476,12 +426,23 @@
         temporal_weight,
     )
     scale = (clips * lax.axis_size("dp") * frames * rows * lax.axis_size("tm") * cols) ** (-0.5)
-    grad = grad.reshape(4, 3, chans, chans)
+    whole = jax.ShapeDtypeStruct((frames, cells, chans), BF16)
+    block_out, lat_grad, spatial, temporal = pl.pallas_call(
+        functools.partial(tail_kernel, scale),
+        out_shape=(
+            whole, whole,
+            jax.ShapeDtypeStruct((3, 3, 8, 32, chans), F32), jax.ShapeDtypeStruct((3, 8, 32, chans), F32),
+        ),
+        in_specs=[vmem_spec] * 3,
+        out_specs=(any_spec,) * 4,
+        scratch_shapes=[pltpu.VMEM((4, 3, 8, 32, chans), F32), pltpu.SemaphoreType.DMA((6,))],
+        compiler_params=pltpu.CompilerParams(vmem_limit_bytes=16 * 1024 * 1024),
+    )(*results)
     return (
         block_out.reshape(latents.shape),
         lat_grad.reshape(latents.shape),
-        grad[:3].astype(F32) * scale,
-        grad[3].astype(F32) * scale,
+        spatial.reshape(3, 3, chans, chans),
+        temporal.reshape(3, chans, chans),
     )
 
 

time: 84.9 us -> 65.4 us (0.77)
  Pallas kernels: 76.4 us -> 64.7 us
  other arithmetic: 5.07 us -> 0 us
  local copies, waits for them, and re-layouts: 2.64 us -> 0 us
    pallas_call x1 -> x2, Pallas kernels: 76.4 us -> 64.7 us  [the longest x1 62.2 us: body(): pl.pallas_call(kernel, out_shape=(half, half, pltpu.VMEM((6, 4, 8, 32, 12...]
    mul x2 -> x0, other arithmetic: 5.07 us -> none  [the longest x1 3.1 us: body(): grad[:3].astype(F32) * scale]
    unnamed x6 -> x0, local copies, waits for them, and re-layouts: 2.64 us -> none
where the time goes in v2:
time: 65.4 us; the launch traced here: 65.3 us
  Pallas kernels  64.7 us (99%)
    pallas_call x1, Pallas kernels, body(): pl.pallas_call(kernel, out_shape=(half, half, pltpu.VMEM((6, 4, 8, 32, 12...  62.2 us
    pallas_call x1, Pallas kernels, body(): pl.pallas_call(functools.partial(tail_kernel, scale), out_shape=(whole, w...  2.44 us

profile of v2, /device:TPU:1, one launch (start us, length us, event | category | flops | bytes accessed | tf_op | source)
XLA Modules:
  0.0 65.3 jit_solution(1818276016290910697)
XLA Ops:
  0.6 62.2 %shard_map.75 = (bf16[17,128,256]{2,1,0:T(8,128)(2,1)S(1)}, bf16[17,128,256]{2,1,0:T(8,128)(2,1)S(1)}, bf16[6,4,8,32,128]{4,3,2,1,0:T(8,128)(2,1)S(1)}) custom-call(bf16[17,2,64,256]{3,2,1,0:T(8,128)(2,1)} %bitcast.6, bf16[17,128,256]{2,1,0:T(8,128)(2,1)} %bitcast.7, bf16[3,3,256,256]{3,2,1,0:T(8,128)(2,1)} %weight.1, bf16[3,256,256]{2,1,0:T(8,128)(2,1)} %mix.1), custom_call_target="tpu_custom_call" | custom-call | tf_op jit(solution)/shard_map/pallas_call | solution.py:398
  62.9 2.4 %shard_map.76 = (bf16[17,128,256]{2,1,0:T(8,128)(2,1)}, bf16[17,128,256]{2,1,0:T(8,128)(2,1)}, f32[3,3,8,32,256]{4,3,2,1,0:T(8,128)}, f32[3,8,32,256]{3,2,1,0:T(8,128)}) custom-call(bf16[17,128,256]{2,1,0:T(8,128)(2,1)S(1)} %get-tuple-element.11.mixed, bf16[17,128,256]{2,1,0:T(8,128)(2,1)S(1)} %get-tuple-element.12.back, ...), custom_call_target="tpu_custom_call" | custom-call | tf_op jit(solution)/shard_map/pallas_call | solution.py:430

commit v3 on v2

--- a/solution.py
+++ b/solution.py
@@ -13,8 +13,12 @@
 FRAMES, COLS, CH = 17, 64, 256
 VMEM_LIMIT = 56 * 1024 * 1024
 PAIRS = FRAMES // 2
-
-CORE, XF, XB, XF2, ZS, YS, ZG, XG, CG, SLOTS = 0, 1, 2, 3, 4, 11, 14, 21, 24, 25
+PARTS = FRAMES - PAIRS
+EARLY = 6
+
+CORE, XF, XB, XF2, ZS, YS, ZG, XG, CG, SLOTS = 0, 1, 2, 3, 4, 11, 14, 21, 24, 28
+SPLIT = 1
+ROWS = 32 // SPLIT
 
 
 def peer(dp, tm):
@@ -36,10 +40,10 @@
         self.x_send, self.x_recv = x_send, x_recv
         self.z_send, self.z_recv, self.y_buf = z_send, z_recv, y_buf
         self.ssem, self.rsem = ssem, rsem
-        self.step = 1 - 2 * self.core
         self.copies = {}
-        self.fwd = lax.rem(self.x + self.step + NX, NX)
-        self.bwd = lax.rem(self.x - self.step + NX, NX)
+        step = 1 - 2 * self.core
+        self.fwd = lax.rem(self.x + step + NX, NX)
+        self.bwd = lax.rem(self.x - step + NX, NX)
         self.far = lax.rem(self.x + 2, NX)
         self.tm = self.z * NY + self.y
 
@@ -69,95 +73,101 @@
         for copy in self.copies.values():
             copy.wait_send()
 
-    def tile(self, s):
-        return self.core * 3 + s
-
     def stages(self, s):
-        return self.x_first(s)
-
-    def core_out(self, s):
-        other = (1 - self.core) * 3 + s
-        self.c_send[s] = self.grads[other].astype(BF16)
-        self.send(s, CORE, self.c_send.at[s], self.c_recv.at[s], self.partner())
-
-    def core_back(self, s):
-        t = self.tile(s)
-        self.send(s, CG, self.total.at[t], self.total.at[t], self.partner())
-
-    def y_out(self, s, value):
-        self.y_buf[s, self.y] = value.astype(BF16)
-        for j in range(1, NY):
-            self.send(s, YS + j - 1, self.y_buf.at[s, self.y], self.y_buf.at[s, self.y], self.at_y(j))
-
-    def y_sum(self, s):
-        self.arrive(s, *range(YS, YS + NY - 1))
-        value = self.y_buf[s, 0].astype(F32)
-        for j in range(1, NY):
-            value = value + self.y_buf[s, j].astype(F32)
-        return value.astype(BF16)
-
-    def x_first(self, s):
-        t = self.tile(s)
-
-        def local(x):
-            return self.grads[t, x] + self.c_recv[s, x].astype(F32)
+        part = s // SPLIT
+        rows = pl.ds(s % SPLIT * ROWS, ROWS)
+        t = self.core * 3 + part
+        other = (1 - self.core) * 3 + part
+        z = self.z
+        x, y = self.x, self.y
+        step = 1 - 2 * self.core
+        fwd, bwd, far = lax.rem(x + step + NX, NX), lax.rem(x - step + NX, NX), lax.rem(x + 2, NX)
+
+        def at_ring(at):
+            return peer(at * 2 + self.core, self.tm)
+
+        def at_cast(j):
+            return self.at_y(j)
+
+        hops = (4, 3, 5, 2, 6, 1, 7)
+
+        def local(at):
+            return self.grads[t, at, :, rows] + self.c_recv[part, at, :, rows].astype(F32)
+
+        def core_out():
+            self.c_send[part, :, :, rows] = self.grads[other, :, :, rows].astype(BF16)
+            self.send(s, CORE, self.c_send.at[part, :, :, rows], self.c_recv.at[part, :, :, rows], self.partner())
+
+        def x_send(kind, value, to):
+            self.x_send[part, kind, :, rows] = value.astype(BF16)
+            self.send(s, XF + kind, self.x_send.at[part, kind, :, rows], self.x_recv.at[part, kind, :, rows], at_ring(to))
+
+        def got(kind):
+            return self.x_recv[part, kind, :, rows].astype(F32)
 
         def first():
             self.arrive(s, CORE)
-            self.x_send[s, 0] = local(self.far).astype(BF16)
-            self.send(s, XF, self.x_send.at[s, 0], self.x_recv.at[s, 0], self.at_x(self.fwd))
-            self.x_send[s, 1] = local(self.bwd).astype(BF16)
-            self.send(s, XB, self.x_send.at[s, 1], self.x_recv.at[s, 1], self.at_x(self.bwd))
+            x_send(0, local(far), fwd)
+            x_send(1, local(bwd), bwd)
 
         def second():
             self.arrive(s, XF)
-            self.x_send[s, 2] = (local(self.fwd) + self.x_recv[s, 0].astype(F32)).astype(BF16)
-            self.send(s, XF2, self.x_send.at[s, 2], self.x_recv.at[s, 2], self.at_x(self.fwd))
+            x_send(2, local(fwd) + got(0), fwd)
 
         def third():
             self.arrive(s, XB, XF2)
-            own = local(self.x) + self.x_recv[s, 1].astype(F32) + self.x_recv[s, 2].astype(F32)
-            self.grads[t, self.x] = own
-            self.z_send[s, 0] = own.astype(BF16)
-            for j in (4, 3, 5, 2, 6, 1, 7):
-                z, device = self.at_z(j)
-                self.send(s, ZS + j - 1, self.z_send.at[s, 0, z], self.z_recv.at[s, j - 1, 0], device)
+            own = local(x) + got(1) + got(2)
+            self.grads[t, x, :, rows] = own
+            self.z_send[part, 0, :, rows] = own.astype(BF16)
+            for j in hops:
+                at, device = self.at_z(j)
+                self.send(s, ZS + j - 1, self.z_send.at[part, 0, at, rows], self.z_recv.at[part, j - 1, 0, rows], device)
 
         def fourth():
             self.arrive(s, *range(ZS, ZS + NZ - 1))
-            own = self.grads[t, self.x, self.z]
+            own = self.grads[t, x, z, rows]
             for j in range(NZ - 1):
-                own = own + self.z_recv[s, j, 0].astype(F32)
-            self.y_out(s, own)
+                own = own + self.z_recv[part, j, 0, rows].astype(F32)
+            self.y_buf[part, y, rows] = own.astype(BF16)
+            for j in range(1, NY):
+                mine = self.y_buf.at[part, y, rows]
+                self.send(s, YS + j - 1, mine, mine, at_cast(j))
 
         def fifth():
-            self.total[t, self.x, self.z] = self.y_sum(s)
-            block = self.total.at[t, self.x, self.z]
-            for j in (4, 3, 5, 2, 6, 1, 7):
+            self.arrive(s, *range(YS, YS + NY - 1))
+            value = self.y_buf[part, 0, rows].astype(F32)
+            for j in range(1, NY):
+                value = value + self.y_buf[part, j, rows].astype(F32)
+            self.total[t, x, z, rows] = value.astype(BF16)
+            block = self.total.at[t, x, z, rows]
+            for j in hops:
                 self.send(s, ZG + j - 1, block, block, self.at_z(j)[1])
 
         def sixth():
             self.arrive(s, *range(ZG, ZG + NZ - 1))
-            self.x_spread(s, lambda x: self.total.at[t, x])
+            mine = self.total.at[t, x, :, rows]
+            self.send(s, XG, mine, mine, at_ring(fwd))
+            self.send(s, XG + 1, mine, mine, at_ring(bwd))
+            self.send(s, CG, mine, mine, self.partner())
 
         def seventh():
-            self.x_forward(s, lambda x: self.total.at[t, x])
+            self.arrive(s, XG)
+            block = self.total.at[t, bwd, :, rows]
+            self.send(s, XG + 2, block, block, at_ring(fwd))
+            self.send(s, CG + 1, block, block, self.partner())
 
         def eighth():
-            self.arrive(s, XG + 1, XG + 2)
-            self.core_back(s)
-
-        return [lambda: self.core_out(s), first, second, third, fourth, fifth, sixth, seventh, eighth, lambda: self.arrive(s, CG)]
-
-    def x_spread(self, s, block):
-        mine = block(self.x)
-        self.send(s, XG, mine, mine, self.at_x(self.fwd))
-        self.send(s, XG + 1, mine, mine, self.at_x(self.bwd))
-
-    def x_forward(self, s, block):
-        self.arrive(s, XG)
-        got = block(self.bwd)
-        self.send(s, XG + 2, got, got, self.at_x(self.fwd))
+            self.arrive(s, XG + 1)
+            block = self.total.at[t, fwd, :, rows]
+            self.send(s, CG + 2, block, block, self.partner())
+            self.arrive(s, XG + 2)
+            block = self.total.at[t, far, :, rows]
+            self.send(s, CG + 3, block, block, self.partner())
+
+        def ninth():
+            self.arrive(s, *range(CG, CG + 4))
+
+        return [core_out, first, second, third, fourth, fifth, sixth, seventh, eighth, ninth]
 
 
 REDUCE_SCRATCH = [
@@ -169,8 +179,8 @@
     pltpu.VMEM((3, 4, 8, 32, 128), BF16),
     pltpu.VMEM((3, 7, 4, 32, 128), BF16),
     pltpu.VMEM((3, 4, 32, 128), BF16),
-    pltpu.SemaphoreType.DMA((3, SLOTS)),
-    pltpu.SemaphoreType.DMA((3, SLOTS)),
+    pltpu.SemaphoreType.DMA((3 * SPLIT, SLOTS)),
+    pltpu.SemaphoreType.DMA((3 * SPLIT, SLOTS)),
 ]
 
 
@@ -183,7 +193,7 @@
     barrier = pltpu.get_barrier_semaphore()
     tm = z * NY + y
     peers = [peer(x * 2 + 1 - core, tm)]
-    peers += [peer(lax.rem(x + j, NX) * 2 + core, tm) for j in (1, NX - 1)]
+    peers += [peer(lax.rem(x + j, NX) * 2 + core, tm) for j in range(1, NX)]
     peers += [peer(x * 2 + core, z * NY + lax.rem(y + j, NY)) for j in range(1, NY)]
     peers += [peer(x * 2 + core, lax.rem(z + j, NZ) * NY + y) for j in range(1, NZ)]
     peers += list(extra)
@@ -210,7 +220,7 @@
 
 def kernel(
     lat, cot, weight, mix, out_b, out_g, total,
-    ext, cotx, actx, agrad, pg3, pgh, w_v, mix_v,
+    ext, cotx, actx, agrad, pg3, pgh, w_v, w_t, mix_v,
     grads, c_send, c_recv, x_send, x_recv, z_send, z_recv, y_buf, ssem, rsem,
     load_sem, halo_s, halo_r, back_s, back_r,
 ):
@@ -255,8 +265,11 @@
         def _(i):
             for copy in make(i, 2 * i, 2):
                 act(copy)
-        for copy in make(PAIRS, FRAMES - 1, 1):
-            act(copy)
+
+        @pl.loop(PAIRS, PARTS)
+        def _(i):
+            for copy in make(i, i + PAIRS, 1):
+                act(copy)
 
     over(halo, lambda copy: copy.start())
 
@@ -276,6 +289,9 @@
 
     grads[...] = jnp.zeros_like(grads)
 
+    for a in range(3):
+        w_t[a] = w_v[a].T
+
     def add_grad(index, value):
         for t in range(6):
             grads[t, index] += value[:, t * 128 : (t + 1) * 128].reshape(8, 32, 128)
@@ -285,6 +301,8 @@
             copy.wait_recv()
         frames = pl.ds(first, size)
         cells = size * 2 * COLS
+        if size == 1:
+            issue(0, EARLY)
 
         @pl.when(tm == 0)
         def _():
@@ -310,11 +328,6 @@
         cots = jnp.concatenate([cotx[pl.ds(first + k, size)].reshape(cells, CH) for k in range(3)], axis=1)
         add_grad(3, dot(act, cots, TN))
 
-    @pl.loop(0, PAIRS)
-    def _(i):
-        chunk(i, 2 * i, 2)
-
-    chunk(PAIRS, FRAMES - 1, 1)
     def issue(low, high):
         if low < min(high, PAIRS):
             @pl.loop(low, min(high, PAIRS))
@@ -322,10 +335,19 @@
                 for copy in grad_halo(i, 2 * i, 2):
                     copy.start()
         if high > PAIRS:
-            for copy in grad_halo(PAIRS, FRAMES - 1, 1):
-                copy.start()
-
-    issue(0, 5)
+            @pl.loop(max(low, PAIRS), high)
+            def _(i):
+                for copy in grad_halo(i, i + PAIRS, 1):
+                    copy.start()
+
+    @pl.loop(0, PAIRS)
+    def _(i):
+        chunk(i, 2 * i, 2)
+
+    @pl.loop(PAIRS, PARTS)
+    def _(i):
+        chunk(i, i + PAIRS, 1)
+
 
     def mix_unit(i, first, size):
         frames = pl.ds(first, size)
@@ -348,7 +370,7 @@
         value = cotx[frames].reshape(cells, CH).astype(F32)
         back = jnp.zeros((cells, CH), F32)
         for a in range(3):
-            back = back + dot(pg3[frames, 2 - a : 4 - a].reshape(cells, 3 * CH), w_v[a], NT)
+            back = back + dot(pg3[frames, 2 - a : 4 - a].reshape(cells, 3 * CH), w_t[a])
         out_g[frames] = (value + back).astype(BF16).reshape(size, 2 * COLS, CH)
 
     def units(unit, low, high):
@@ -357,18 +379,21 @@
             def _(i):
                 unit(i, 2 * i, 2)
         if high > PAIRS:
-            unit(PAIRS, FRAMES - 1, 1)
+            @pl.loop(max(low, PAIRS), high)
+            def _(i):
+                unit(i, i + PAIRS, 1)
 
     reduce = Reduce(here, grads, total, c_send, c_recv, x_send, x_recv, z_send, z_recv, y_buf, ssem, rsem)
-    steps = [reduce.stages(s) for s in range(3)]
+    steps = [reduce.stages(s) for s in range(3 * SPLIT)]
+    events = [(s, k) for k in range(10) for s in range(3 * SPLIT)]
     filler = {0: (mix_unit, 0, 3), 1: (mix_unit, 3, 9), 3: (back_unit, 0, 3), 5: (back_unit, 3, 5), 7: (back_unit, 5, 7), 8: (back_unit, 7, 9)}
-    for stage in range(10):
-        for s in range(3):
-            steps[s][stage]()
-        if stage == 5:
-            issue(5, 9)
-        if stage in filler:
-            units(*filler[stage])
+    for s, stage in events:
+        steps[s][stage]()
+        if s == 3 * SPLIT - 1:
+            if stage == 5:
+                issue(EARLY, PARTS)
+            if stage in filler:
+                units(*filler[stage])
 
     reduce.finish()
     over(halo, lambda copy: copy.wait_send())
@@ -408,13 +433,14 @@
             pltpu.VMEM((frames, 4, cols, 3 * chans), BF16),
             pltpu.VMEM((2, frames, cols, chans), BF16),
             pltpu.VMEM((3, chans, 3 * chans), BF16),
+            pltpu.VMEM((3, 3 * chans, chans), BF16),
             pltpu.VMEM((3, chans, chans), BF16),
             *REDUCE_SCRATCH,
             pltpu.SemaphoreType.DMA((12,)),
-            pltpu.SemaphoreType.DMA((2, PAIRS + 1)),
-            pltpu.SemaphoreType.DMA((2, PAIRS + 1)),
-            pltpu.SemaphoreType.DMA((2, PAIRS + 1)),
-            pltpu.SemaphoreType.DMA((2, PAIRS + 1)),
+            pltpu.SemaphoreType.DMA((2, PARTS)),
+            pltpu.SemaphoreType.DMA((2, PARTS)),
+            pltpu.SemaphoreType.DMA((2, PARTS)),
+            pltpu.SemaphoreType.DMA((2, PARTS)),
         ],
         compiler_params=pltpu.CompilerParams(
             collective_id=0, has_side_effects=True, vmem_limit_bytes=VMEM_LIMIT

time: 65.4 us -> 65.3 us (level)
  no operation moved by 1% of the time
where the time goes in v3:
time: 65.3 us; the launch traced here: 65.2 us
  Pallas kernels  64.6 us (99%)
    pallas_call x1, Pallas kernels, body(): pl.pallas_call(kernel, out_shape=(half, half, pltpu.VMEM((6, 4, 8, 32, 12...  62.1 us
    pallas_call x1, Pallas kernels, body(): pl.pallas_call(functools.partial(tail_kernel, scale), out_shape=(whole, w...  2.44 us

profile of v3, /device:TPU:1, one launch (start us, length us, event | category | flops | bytes accessed | tf_op | source)
XLA Modules:
  0.0 65.2 jit_solution(9747967943449732550)
XLA Ops:
  0.6 62.1 %shard_map.75 = (bf16[17,128,256]{2,1,0:T(8,128)(2,1)S(1)}, bf16[17,128,256]{2,1,0:T(8,128)(2,1)S(1)}, bf16[6,4,8,32,128]{4,3,2,1,0:T(8,128)(2,1)S(1)}) custom-call(bf16[17,2,64,256]{3,2,1,0:T(8,128)(2,1)} %bitcast.6, bf16[17,128,256]{2,1,0:T(8,128)(2,1)} %bitcast.7, bf16[3,3,256,256]{3,2,1,0:T(8,128)(2,1)} %weight.1, bf16[3,256,256]{2,1,0:T(8,128)(2,1)} %mix.1), custom_call_target="tpu_custom_call" | custom-call | tf_op jit(solution)/shard_map/pallas_call | solution.py:423
  62.8 2.4 %shard_map.76 = (bf16[17,128,256]{2,1,0:T(8,128)(2,1)}, bf16[17,128,256]{2,1,0:T(8,128)(2,1)}, f32[3,3,8,32,256]{4,3,2,1,0:T(8,128)}, f32[3,8,32,256]{3,2,1,0:T(8,128)}) custom-call(bf16[17,128,256]{2,1,0:T(8,128)(2,1)S(1)} %get-tuple-element.11.mixed, bf16[17,128,256]{2,1,0:T(8,128)(2,1)S(1)} %get-tuple-element.12.back, ...), custom_call_target="tpu_custom_call" | custom-call | tf_op jit(solution)/shard_map/pallas_call | solution.py:456
